TPU v7x, 32 devices: a whole 2x2x4 slice. The times are simulated.
32 devices in a mesh: patch: 8 (over y, x, core), grp: 4 (over z).
Axes of the slice: x: 2, y: 2, z: 4, core: 2. Of those that a mesh axis runs over, the one named last changes fastest.
Arguments:
- cells: int32 [3, 8, 4, 32, 128], P(None, 'patch', 'grp'), may hold values from 0 to 15, as said below
- offsets: float32 [3, 8, 4, 32, 128], P(None, 'patch', 'grp'), may hold values from -0.5 to 0.5
- charges: float32 [8, 4, 32, 128], P('patch', 'grp'), may hold values from -4 to 4
- masses: float32 [8, 4, 32, 128], P('patch', 'grp'), may hold values from 1 to 16
- velocity: float32 [3, 8, 4, 32, 128], P(None, 'patch', 'grp'), may hold values from -5 to 5
- task_first: int32 [8, 4, 32], P('patch', 'grp'), may hold values from 0 to 127, as said below
- task_second: int32 [8, 4, 32], P('patch', 'grp'), may hold values from 0 to 255, as said below
- task_count: int32 [8, 4], P('patch', 'grp'), may hold values from 0 to 32, as said below
- kernel_taps: float32 [6, 17], replicated, may hold values from -3 to 3
Outputs:
- displacement: float32 [3, 8, 4, 32, 128], P(None, 'patch', 'grp')
- velocities: float32 [3, 8, 4, 32, 128], P(None, 'patch', 'grp')
Inputs may be any that keep to these rules, and one draw needn't show every extreme that they name: `cells`: components x, y, z lie below 8, 16, 8. `task_first`: A patch of the host's slab, written strip * 32 + place. `task_second`: slab step * 4 * 32 + strip * 32 + place of one of the 13 forward neighbours of the first patch, periodic: in the next slab any of the 9 with strip and place within one; in the same slab strip + 0 with place + 1, or strip + 1 with place within one. A pair may repeat. `task_count`: on each slab the 4 counts add up to exactly 64; every slab has one device with 32 live slots and one with none. Slots at or past the count are ignored.
All inputs are finite; a program needn't handle non-finite values.
Results may differ from a plain program's by a relative error of at most 0.000068.
Values sent between devices are 32-bit elements; how exact they have to be, the bound alone decides.
No kernel may reach another device: no remote copies, remote signals or barrier semaphores. Data moves between devices by JAX's collectives and lax.ppermute only.
A program may use at most 64 MiB of HBM per device.

v0:
```python
import functools

import jax
import jax.numpy as jnp
from jax import lax
from jax.experimental import pallas as pl
from jax.experimental.pallas import tpu as pltpu
from jax.sharding import PartitionSpec as P


MXD = 8
MYD = 16
PZ = 8
RADIUS = 8

time_step = 0.5
soft_end = 65.0
push_scale = 1.0 / 4096.0

XO = MXD + 2
YO = MYD + 2
YR = 24
XW = XO + 2 * RADIUS
YE = RADIUS + 2
NE = 104
NS = 184
N2 = 40

UNROLL = 8


f32 = jnp.float32
bf16 = jnp.bfloat16
i32 = jnp.int32


def split(x):
    hi = x.astype(bf16)
    lo = (x - hi.astype(f32)).astype(bf16)
    return hi, lo


def dot(a, b, dims=(((1,), (0,)), ((), ()))):
    return lax.dot_general(a, b, dims, preferred_element_type=f32)


def dot3(a, b, dims=(((1,), (0,)), ((), ()))):
    ah, al = a
    bh, bl = b
    return dot(ah, bh, dims) + (dot(al, bh, dims) + dot(ah, bl, dims))


NT = (((1,), (1,)), ((), ()))
TN = (((0,), (0,)), ((), ()))


def iota(shape, dim):
    return lax.broadcasted_iota(i32, shape, dim)


def spline(frac):
    weights = (0.5 * (0.5 - frac) ** 2, 0.75 - frac * frac, 0.5 * (0.5 + frac) ** 2)
    slopes = (frac - 0.5, -2.0 * frac, 0.5 + frac)
    return weights, slopes


def place3(rows, base, values):
    out = jnp.where(rows == base, values[0], 0.0)
    out = jnp.where(rows == base + 1, values[1], out)
    return jnp.where(rows == base + 2, values[2], out)


def pair_rows(ref, c, m):
    if c is None:
        return jnp.concatenate([ref[2 * m : 2 * m + 1, :], ref[2 * m + 1 : 2 * m + 2, :]], axis=1)
    return jnp.concatenate([ref[c, 2 * m : 2 * m + 1, :], ref[c, 2 * m + 1 : 2 * m + 2, :]], axis=1)


def fill_spline(store, frac, c, slopes):
    places = frac.shape[1]
    weights, derivs = spline(frac[c])
    for n, value in enumerate(weights + derivs if slopes else weights):
        at = (6 * c + n) * places
        store[at : at + places, :] = value


def pair_values(store, places, c, m, first):
    out = []
    for n in range(first, first + 3):
        at = (6 * c + n) * places + 2 * m
        out.append(jnp.concatenate([store[at : at + 1, :], store[at + 1 : at + 2, :]], axis=1))
    return out


def pair_base_z(cz, atoms):
    second = (iota(cz.shape, 1) >= atoms).astype(i32)
    return cz + (PZ - 1) + PZ * second


def list_block(first, second, count, places, strips, lanes):
    bits = places.bit_length() - 1
    slots = first.shape[1]
    live = iota((1, slots), 1) < count
    upper = (second >= places * strips).astype(i32)
    rest = second - upper * (places * strips)
    dead = jnp.full((1, lanes - slots), -1.0, f32)
    rows = [
        jnp.where(live, first >> bits, -1),
        first & (places - 1),
        jnp.where(live, rest >> bits, -1),
        rest & (places - 1),
        upper,
    ]
    rows = [jnp.concatenate([row.astype(f32), dead], axis=1) for row in rows]
    return jnp.concatenate(rows + [jnp.zeros((3, lanes), f32)], axis=0)


def spread_kernel(*refs, strips):
    sources, count, outs, scratch = refs[:6], refs[6], refs[7:13], refs[13:]
    own, pk_lo, pk_hi, pos, lists, taps_out = outs
    cells, frac, charge, first, second, taps, acc, sem, store = scratch
    copies = [
        pltpu.make_async_copy(src, dst, sem.at[n])
        for n, (src, dst) in enumerate(zip(sources, scratch[:6]))
    ]
    for copy in copies:
        copy.start()
    acc[...] = jnp.zeros_like(acc)
    pk_lo[0 : 2 * NE, :] = jnp.zeros((2 * NE, 128), f32)
    pk_hi[0 : 2 * NE, :] = jnp.zeros((2 * NE, 128), f32)
    for copy in copies:
        copy.wait()
    places, atoms = charge.shape
    depth = places * PZ
    for c in range(3):
        start = cells[c].astype(f32) + frac[c]
        for dst, at in ((pos, 0), (pk_lo, 2 * NE), (pk_hi, 2 * NE)):
            dst[at + c * places : at + (c + 1) * places, :] = start
    taps_out[...] = jnp.zeros_like(taps_out)
    taps_out[0 : taps.shape[0], 0 : taps.shape[1]] = taps[...]
    q = charge[...]
    for dst, at in ((pos, 0), (pk_lo, 2 * NE), (pk_hi, 2 * NE)):
        dst[at + 3 * places : at + 4 * places, :] = q
    block = list_block(first[...], second[...], count[0, 0], places, strips, atoms)
    at = 2 * NE + 4 * places
    lists[...] = block
    pk_lo[at : at + 8, :] = block
    pk_hi[at : at + 8, :] = block
    for c in range(3):
        fill_spline(store, frac, c, False)
    y_rows = iota((YR, 2 * atoms), 0)
    x_rows = iota((16, 2 * atoms), 0)
    z_rows = iota((4 * PZ, 2 * atoms), 0)
    for m in range(places // 2):
        wx = place3(x_rows, pair_rows(cells, 0, m), pair_values(store, places, 0, m, 0))
        wy = place3(y_rows, pair_rows(cells, 1, m), pair_values(store, places, 1, m, 0))
        bz = pair_base_z(pair_rows(cells, 2, m), atoms)
        wz = place3(z_rows, bz, pair_values(store, places, 2, m, 0))
        wy = wy * pair_rows(charge, None, m)
        table = jnp.concatenate([wx[x : x + 1, :] * wy for x in range(XO)], axis=0)
        rows = pl.ds(2 * PZ * m, 4 * PZ)
        wh, wl = split(wz)
        th, tl = split(table)
        acc[rows, : XO * YR] += dot(
            jnp.concatenate([wh, wl, wh], axis=1), jnp.concatenate([th, th, tl], axis=1), NT
        )
    acc[depth : depth + PZ, :] += acc[0:PZ, :]
    acc[PZ : 2 * PZ, :] += acc[depth + PZ : depth + 2 * PZ, :]
    grid = jnp.transpose(acc[PZ : PZ + depth, :])
    own[...] = grid[: XO * YR, :]
    for x in range(XO):
        for half in range(2):
            dst = pl.ds(half * NE + x * YE, YE)
            lanes = slice(half * 128, half * 128 + 128)
            pk_lo[dst, :] = own[x * YR : x * YR + YE, lanes]
            pk_hi[dst, :] = own[x * YR + YO - YE : x * YR + YO, lanes]


def fill_receivers(parts, posr, places):
    rows = iota((8, 128), 0)
    for c in range(3):
        base = 8 * (places + 1) * c
        constant = jnp.where(rows == c, -1.0, 0.0)
        for r in range(places + 1):
            parts[base + 8 * r : base + 8 * r + 8, :] = constant
        for g in range(0, places, 8):
            x = posr[c * places + g : c * places + g + 8, :]
            hi = x.astype(bf16).astype(f32)
            rest = x - hi
            mid = rest.astype(bf16).astype(f32)
            for n, value in enumerate((hi, mid, rest - mid)):
                parts[pl.ds(base + 8 * g + 4 + n, 8, stride=8), :] = value


def side_operands(parts, src, source, r, shifts):
    rows = iota((8, 128), 0)
    shift_x, shift_y, shift_z = shifts
    shift = jnp.where(rows == 0, shift_x, jnp.where(rows == 1, shift_y, shift_z))
    at = src[pl.ds(pl.multiple_of(8 * source, 8), 8), :]
    at = jnp.where(rows < 3, at - shift, at)
    hi = at.astype(bf16).astype(f32)
    rest = at - hi
    mid = rest.astype(bf16).astype(f32)
    low = rest - mid
    mid = pltpu.roll(mid, 4, 0)
    left = jnp.concatenate(
        [jnp.where(rows < 4, hi, mid), jnp.where(rows < 4, low, 1.0)], axis=0
    )
    top = []
    end = []
    for c in range(4):
        sign = 1.0 if c == 3 else -1.0
        top.append(jnp.where((rows & 3) == c, sign, 0.0))
        if c < 3:
            end.append(parts[pl.ds(pl.multiple_of(parts.shape[0] // 3 * c + 8 * r, 8), 8), :])
        else:
            end.append(jnp.where(rows == c, sign, 0.0))
    right = jnp.concatenate(
        [jnp.concatenate(top, axis=1), jnp.concatenate(end, axis=1)], axis=0
    )
    return jnp.transpose(left).astype(bf16), right.astype(bf16)


def side_push(force, pairs, r):
    shape = (8, 128)
    ax = jnp.zeros(shape, f32)
    ay = jnp.zeros(shape, f32)
    az = jnp.zeros(shape, f32)
    for k in range(16):
        rows = slice(8 * k, 8 * k + 8)
        dx = pairs[rows, 0:128]
        dy = pairs[rows, 128:256]
        dz = pairs[rows, 256:384]
        qs = pairs[rows, 384:512]
        soft = (dx * dx + dy * dy) + (dz * dz + 1.0)
        reach = jnp.maximum(soft_end - soft, 0.0)
        rs = lax.rsqrt(soft)
        t = reach * rs
        c = (t * t) * (rs * qs)
        ax = ax + c * dx
        ay = ay + c * dy
        az = az + c * dz
    for c, a in enumerate((ax, ay, az)):
        rows = pl.ds(pl.multiple_of((3 * r + c) * 8, 8), 8)
        force[rows, :] += a


def add_sides(force, parts, src, pairs, number, places, decode):
    def prepare(n, dst):
        r, source, shifts = decode(n)
        left, right = side_operands(parts, src, source, r, shifts)
        dst[...] = dot(left, right)

    def receiver(n):
        return jnp.where(n < number, decode(n)[0], places)

    def body(m, carry):
        n = UNROLL * m
        for u, dst in enumerate(pairs):
            prepare(n + u, dst)
        for u, dst in enumerate(pairs):
            side_push(force, dst, receiver(n + u))
        return carry

    lax.fori_loop(0, (number + UNROLL - 1) // UNROLL, body, 0)


def fill_sources(src, block, component, places):
    for c in range(4):
        rows = component(c)
        for g in range(0, places, 8):
            at = (block * places + g) * 8 + c
            src[pl.ds(at, 8, stride=8), :] = rows[g : g + 8, :]


def rows_of(ref, begin, places):
    return lambda c: ref[begin + c * places : begin + (c + 1) * places, :]


def moved_rows(ref, begin, charges, at, places):
    return lambda c: (
        charges[at + 3 * places : at + 4 * places, :]
        if c == 3
        else ref[begin + c * places : begin + (c + 1) * places, :]
    )


def folded_force(force, posr, places):
    part = force[0 : 24 * places, :].reshape(places, 3, 8, 128)
    total = jnp.sum(part, axis=2)
    scale = posr[3 * places : 4 * places, :] * push_scale
    return [total[:, c, :] * scale for c in range(3)]


def add_self(force, parts, src, pairs, places):
    def decode(n):
        n = jnp.minimum(n, places - 1)
        return n, n, (0.0, 0.0, 0.0)

    add_sides(force, parts, src, pairs, places, places, decode)


def add_listed(force, parts, src, pairs, work, places, across, begin, end):
    bits = places.bit_length() - 1

    def decode(n):
        code = work[0, begin + n]
        r = code & (places - 1)
        source = code >> bits
        p = source & (places - 1)
        strip = source >> bits
        slab = jnp.int32(0)
        if across:
            slab = jnp.where(strip >= 3, 1, -1)
            strip = jnp.where(strip >= 3, strip - 3, strip)
        dz = ((r - p + 1) & (places - 1)) - 1
        shifts = (
            (-MXD * slab).astype(f32),
            (-MYD * (strip - 1)).astype(f32),
            (PZ * dz).astype(f32),
        )
        return r, source, shifts

    add_sides(force, parts, src, pairs, end - begin, places, decode)


def wrap_step(delta, count):
    return jnp.where(delta > 1, delta - count, jnp.where(delta < -1, delta + count, delta))


def join_lists(blocks, slots, strips):
    lane = iota((8, 128), 1)
    group = 128 // slots
    parts = []
    for g in range(0, strips, group):
        joined = blocks[g]
        for n in range(1, group):
            block = pltpu.roll(blocks[g + n], n * slots, 1) if g + n < strips else -1.0
            joined = jnp.where(lane < n * slots, joined, block)
        parts.append(joined)
    return parts


def compact(work, mask, early, source, receiver, places):
    size = mask.shape[1]
    wide = work.shape[1]
    first = jnp.where(mask & early, 1.0, 0.0)
    rest = jnp.where(mask, 1.0, 0.0) - first
    rows = iota((8, size), 0)
    before = jnp.where(iota((size, size), 0) < iota((size, size), 1), 1.0, 0.0).astype(bf16)
    rank = dot(jnp.where(rows == 0, first, rest).astype(bf16), before)
    firsts = jnp.sum(first, axis=1, keepdims=True)
    number = firsts + jnp.sum(rest, axis=1, keepdims=True)
    rank = jnp.where(first > 0.5, rank[0:1], firsts + rank[1:2]).astype(i32)
    rank = jnp.where(mask, rank, -1)
    chosen = jnp.where(iota((wide, size), 0) == rank, 1.0, 0.0).astype(bf16)
    values = jnp.where(rows == 0, jnp.where(mask, source, 0.0), jnp.where(rows == 1, receiver, 0.0))
    got = dot(values.astype(bf16), chosen, NT)
    code = (got[0:1] * places + got[1:2]).astype(i32)
    rows = iota((8, wide), 0)
    counts = jnp.where(rows == 1, number.astype(i32), firsts.astype(i32))
    work[...] = jnp.where(rows == 0, code, counts)


def list_near(work, tables, places, strips):
    t = jnp.concatenate(tables, axis=1)
    mine = lax.axis_index("grp").astype(f32)
    a, pa, b, pb, upper = (t[n : n + 1] for n in range(5))
    left = (a == mine) & (upper == 0.0)
    right = (b == mine) & (upper == 0.0)
    mask = jnp.concatenate([jnp.where(left, 1.0, 0.0), jnp.where(right, 1.0, 0.0)], axis=1) > 0.5
    both = (
        mask,
        mask,
        jnp.concatenate(
            [
                (wrap_step(b - mine, strips) + 1.0) * places + pb,
                (wrap_step(a - mine, strips) + 1.0) * places + pa,
            ],
            axis=1,
        ),
        jnp.concatenate([pa, pb], axis=1),
    )
    compact(work, *both, places)


def list_across(work, tables, tables_below, places, strips):
    t, u = jnp.concatenate(tables, axis=1), jnp.concatenate(tables_below, axis=1)
    mine = lax.axis_index("grp").astype(f32)
    left = (t[0:1] == mine) & (t[4:5] == 1.0)
    right = (u[2:3] == mine) & (u[4:5] == 1.0)
    both = (
        jnp.concatenate([jnp.where(left, 1.0, 0.0), jnp.where(right, 1.0, 0.0)], axis=1) > 0.5,
        jnp.concatenate([t[2:3], u[0:1]], axis=1) == mine,
        jnp.concatenate(
            [
                (wrap_step(t[2:3] - mine, strips) + 4.0) * places + t[3:4],
                (wrap_step(u[0:1] - mine, strips) + 1.0) * places + u[1:2],
            ],
            axis=1,
        ),
        jnp.concatenate([t[1:2], u[3:4]], axis=1),
    )
    compact(work, *both, places)


def tables_of(column, places):
    begin = 12 * places
    return [column[at : at + 8, :] for at in range(begin, column.shape[0], 8)]


def column_kernel(*refs, number_far, strips, slots):
    up, down, pos, lists = refs[:4]
    far = refs[4 : 4 + number_far]
    column = refs[-1]
    rows = pos.shape[0]
    for n, (src, begin) in enumerate(((down, 2 * NE), (pos, 0), (up, 2 * NE))):
        column[n * rows : (n + 1) * rows, :] = src[begin : begin + rows, :]
    at = 2 * NE + rows
    blocks = [lists[...], down[at : at + 8, :], up[at : at + 8, :]] + [r[...] for r in far]
    for n, table in enumerate(join_lists(blocks, slots, strips)):
        column[3 * rows + 8 * n : 3 * rows + 8 * n + 8, :] = table


def tap_lookup(taps, t, index):
    span = 2 * RADIUS + 1
    index = jnp.where((index >= 0) & (index < span), index, 127)
    row = jnp.broadcast_to(taps[t : t + 1, :], (8, 128))
    blocks = []
    for i in range(0, index.shape[0], 8):
        blocks.append(
            jnp.concatenate(
                [
                    jnp.take_along_axis(row, index[i : i + 8, j : j + 128], axis=1)
                    for j in range(0, index.shape[1], 128)
                ],
                axis=1,
            )
        )
    return jnp.concatenate(blocks, axis=0)


def line_table(taps, t, depth):
    half = depth // 2
    rows, lanes = iota((half, half), 0), iota((half, half), 1)
    same = tap_lookup(taps, t, lanes - rows + RADIUS)
    other = tap_lookup(taps, t, (lanes - rows + half + RADIUS) % depth)
    return jnp.concatenate(
        [jnp.concatenate([same, other], axis=1), jnp.concatenate([other, same], axis=1)], axis=0
    )


def plane_table(taps, t, x_of, y_of):
    lanes = x_of.shape[1]
    x_rows = iota((32, lanes), 0) - (RADIUS + 1)
    y_rows = iota((YR, lanes), 0) - 1
    along_x = tap_lookup(taps, t, x_rows - x_of + RADIUS)
    along_y = tap_lookup(taps, t, y_rows - y_of + RADIUS)
    return jnp.concatenate([along_x[x : x + 1, :] * along_y for x in range(XW)], axis=0)


def put_split(pair, rows, lanes, value):
    hi, lo = split(value)
    pair[0, rows, lanes] = hi
    pair[1, rows, lanes] = lo


def tables_kernel(
    taps, own, pos, line, edge_table, partial, force_out, parts, table, smooth, src, *pairs
):
    places = pos.shape[0] // 4
    depth = places * PZ
    terms = line.shape[1]
    lane_own = iota((8, 256), 1)
    own_x = lane_own[0:1] // YR - 1
    own_y = lane_own[0:1] % YR - 1
    own_x = jnp.where(lane_own[0:1] < XO * YR, own_x, 1000)
    lane = iota((1, 256), 1)
    in_up = lane < XO * YE
    in_down = (lane >= NE) & (lane < NE + XO * YE)
    local = jnp.where(in_up, lane, lane - NE)
    edge_x = jnp.where(in_up | in_down, local // YE - 1, 1000)
    edge_y = local % YE + jnp.where(in_up, MYD - 1, -(RADIUS + 1))
    own_pair = split(jnp.concatenate([own[...], jnp.zeros((16, depth), f32)], axis=0))
    for t in range(terms):
        kz = line_table(taps, t, depth)
        kh, kl = split(kz)
        line[0, t] = kh
        line[1, t] = kl
        q = dot3(own_pair, (kh, kl))
        put_split(smooth, slice(t * 256, t * 256 + 256), slice(None), q)
        put_split(table, slice(None), slice(t * 256, t * 256 + 256), plane_table(taps, t, own_x, own_y))
        put_split(
            edge_table, slice(None), slice(t * 256, t * 256 + 256), plane_table(taps, t, edge_x, edge_y)
        )
    partial[...] = dot3((table[0], table[1]), (smooth[0], smooth[1]))
    fill_sources(src, 0, rows_of(pos, 0, places), places)
    fill_receivers(parts, pos, places)
    force_out[...] = jnp.zeros_like(force_out)
    add_self(force_out, parts, src, pairs, places)


def planes_kernel(up, down, line, edge_table, partial, pk_lo, pk_hi, e_lo, e_hi, mid, smooth):
    terms = line.shape[1]
    block = jnp.concatenate(
        [jnp.concatenate([src[0:NE, :], src[NE : 2 * NE, :]], axis=1) for src in (up, down)], axis=0
    )
    pair = split(block)
    for t in range(terms):
        q = dot3(pair, (line[0, t], line[1, t]))
        put_split(smooth, slice(t * 256, t * 256 + 2 * NE), slice(None), q)
        for n in range(2):
            smooth[n, t * 256 + 2 * NE : t * 256 + 256, :] = jnp.zeros((256 - 2 * NE, q.shape[1]), bf16)
    total = partial[...] + dot3((edge_table[0], edge_table[1]), (smooth[0], smooth[1]))
    mid[...] = total[RADIUS * YR : (RADIUS + XO) * YR, :]
    low = total[: XO * YR, :]
    high = total[2 * RADIUS * YR :, :]
    for half in range(2):
        lanes = slice(half * 128, half * 128 + 128)
        for x in range(XO):
            rows = pl.ds(half * NS + x * YO, YO)
            pk_lo[rows, :] = low[x * YR : x * YR + YO, lanes]
            pk_hi[rows, :] = high[x * YR : x * YR + YO, lanes]
        for x in range(2):
            rows = pl.ds(half * N2 + x * YO, YO)
            e_lo[rows, :] = low[x * YR : x * YR + YO, lanes]
            e_hi[rows, :] = high[(XO - 2 + x) * YR : (XO - 2 + x) * YR + YO, lanes]
        for dst, size, pad in ((pk_lo, NS, NS - XO * YO), (pk_hi, NS, NS - XO * YO), (e_lo, N2, N2 - 2 * YO), (e_hi, N2, N2 - 2 * YO)):
            dst[(half + 1) * size - pad : (half + 1) * size, :] = jnp.zeros((pad, 128), f32)


def near_kernel(column, pos, force_in, parts, force_out, work_out, work, src, sem, *pairs, strips):
    places = pos.shape[0] // 4
    rows = 4 * places
    list_near(work_out, tables_of(column, places), places, strips)
    copy = pltpu.make_async_copy(work_out, work, sem)
    copy.start()
    force_out[...] = force_in[...]
    for n in range(3):
        fill_sources(src, n, rows_of(column, n * rows, places), places)
    copy.wait()
    add_listed(force_out, parts, src, pairs, work, places, False, 0, work[1, 0])


def sample_kernel(
    cells, frac, charge, masses, velocity, pos, force, mid, low, high, e_lo, e_hi,
    half_out, moved, long, grid, turned, store
):
    places, atoms = charge.shape
    depth = places * PZ
    for c in range(3):
        fill_spline(store, frac, c, True)
    grid[...] = jnp.zeros_like(grid)
    for x in range(XO):
        for half in range(2):
            lanes = slice(half * 128, half * 128 + 128)
            at_x = pl.ds(half * NS + x * YO, YO)
            value = mid[x * YR : x * YR + YO, lanes] + low[at_x, :] + high[at_x, :]
            if x < 2:
                value = value + e_lo[pl.ds(half * N2 + x * YO, YO), :]
            if x >= XO - 2:
                value = value + e_hi[pl.ds(half * N2 + (x - XO + 2) * YO, YO), :]
            grid[x * YR : x * YR + YO, lanes] = value
    body = jnp.transpose(grid[...])
    turned[PZ : PZ + depth, :] = body
    turned[0:PZ, :] = body[depth - PZ :, :]
    turned[PZ + depth : 2 * PZ + depth, :] = body[0:PZ, :]
    y_rows = iota((YR, 2 * atoms), 0)
    x_rows = iota((16, 2 * atoms), 0)
    z_rows = iota((4 * PZ, 2 * atoms), 0)
    for m in range(places // 2):
        vx, dx = pair_values(store, places, 0, m, 0), pair_values(store, places, 0, m, 3)
        vy, dy = pair_values(store, places, 1, m, 0), pair_values(store, places, 1, m, 3)
        vz, dz = pair_values(store, places, 2, m, 0), pair_values(store, places, 2, m, 3)
        bx, by = pair_rows(cells, 0, m), pair_rows(cells, 1, m)
        bz = pair_base_z(pair_rows(cells, 2, m), atoms)
        wx, sx = place3(x_rows, bx, vx), place3(x_rows, bx, dx)
        wy, sy = place3(y_rows, by, vy), place3(y_rows, by, dy)
        both = jnp.concatenate([place3(z_rows, bz, vz), place3(z_rows, bz, dz)], axis=1)
        bh, bl = split(both)
        th, tl = split(turned[2 * PZ * m : 2 * PZ * m + 4 * PZ, :])
        sampled = dot(
            jnp.concatenate([th, th, tl], axis=0), jnp.concatenate([bh, bl, bh], axis=0), TN
        )
        shape = (YR, 2 * atoms)
        gx, gy, gz = jnp.zeros(shape, f32), jnp.zeros(shape, f32), jnp.zeros(shape, f32)
        for x in range(XO):
            plain = sampled[x * YR : (x + 1) * YR, : 2 * atoms]
            sloped = sampled[x * YR : (x + 1) * YR, 2 * atoms :]
            gx = gx + sx[x : x + 1, :] * plain
            gy = gy + wx[x : x + 1, :] * plain
            gz = gz + wx[x : x + 1, :] * sloped
        for c, value in enumerate((gx * wy, gy * sy, gz * wy)):
            line = jnp.sum(value, axis=0, keepdims=True)
            long[c, 2 * m : 2 * m + 1, :] = line[:, :atoms]
            long[c, 2 * m + 1 : 2 * m + 2, :] = line[:, atoms:]
    inverse = time_step * (1.0 / masses[...])
    q = charge[...]
    short = folded_force(force, pos, places)
    for c in range(3):
        total = short[c] - 2.0 * q * long[c]
        half = velocity[c] + inverse * total
        half_out[c] = half
        moved[c * places : (c + 1) * places, :] = (
            pos[c * places : (c + 1) * places, :] + time_step * half
        )


def far_kernel(
    column, below, above, force_in, parts, force, work_out, work, src, sem, *pairs, strips, places
):
    rows = 4 * places
    list_across(work_out, tables_of(column, places), tables_of(below, places), places, strips)
    copy = pltpu.make_async_copy(work_out, work, sem)
    copy.start()
    for n in range(6):
        fill_sources(src, n, rows_of((below, above)[n // 3], n % 3 * rows, places), places)
    force[...] = force_in[...]
    copy.wait()
    add_listed(force, parts, src, pairs, work, places, True, 0, work[1, 0])


def moved_self_kernel(moved, pos, force_out, parts, src, *pairs):
    places = pos.shape[0] // 4
    fill_sources(src, 0, moved_rows(moved, 0, pos, 0, places), places)
    fill_receivers(parts, moved, places)
    force_out[...] = jnp.zeros_like(force_out)
    add_self(force_out, parts, src, pairs, places)


def moved_near_kernel(
    moved, below_strip, above_strip, low, high, charged, below, above, force_in, parts, work, work_across,
    force_out, src, src_across, *pairs
):
    places = moved.shape[0] // 3
    force_out[...] = force_in[...]
    for n, part in enumerate((below_strip, moved, above_strip)):
        fill_sources(src, n, moved_rows(part, 0, charged, 4 * places * n, places), places)
    for n, part, charges in ((1, low, below), (4, high, above)):
        fill_sources(src_across, n, moved_rows(part, 0, charges, 4 * places, places), places)
    add_listed(force_out, parts, src, pairs, work, places, False, 0, work[1, 0])
    add_listed(force_out, parts, src_across, pairs, work_across, places, True, 0, work_across[2, 0])


def moved_far_kernel(
    low, high, pos, below, above, force_in, parts, work, half, masses,
    shown, speed, force, src, *pairs
):
    places = pos.shape[0] // 4
    force[...] = force_in[...]
    for n in range(2):
        part, charged = ((low, below), (high, above))[n]
        for k in range(2):
            block = moved_rows(part, 3 * places * k, charged, 8 * places * k, places)
            fill_sources(src, 3 * n + 2 * k, block, places)
    add_listed(force, parts, src, pairs, work, places, True, work[2, 0], work[1, 0])
    short = folded_force(force, pos, places)
    inverse = time_step * (1.0 / masses[...])
    for c in range(3):
        before = half[c]
        after = before + inverse * short[c]
        speed[c] = after
        shown[c] = time_step * (before + after)


def call(kernel, outs, scratch, *args, flops=0, smem=(), hbm=()):
    def space(n):
        return pltpu.SMEM if n in smem else pltpu.HBM if n in hbm else pltpu.VMEM

    return pl.pallas_call(
        kernel,
        out_shape=outs,
        in_specs=[pl.BlockSpec(memory_space=space(n)) for n in range(len(args))],
        out_specs=[pl.BlockSpec(memory_space=pltpu.VMEM)] * len(outs),
        scratch_shapes=scratch,
        cost_estimate=pl.CostEstimate(flops=flops, transcendentals=0, bytes_accessed=1 << 20),
        compiler_params=pltpu.CompilerParams(vmem_limit_bytes=20 * 1024 * 1024),
    )(*args)


def shifted(x, axis, distance):
    size = lax.axis_size(axis)
    return lax.ppermute(x, axis, [(i, (i + distance) % size) for i in range(size)])


def step(
    cells, offsets, charges, masses, velocity, task_first, task_second, task_count, kernel_taps
):
    cells, offsets, velocity = cells[:, 0, 0], offsets[:, 0, 0], velocity[:, 0, 0]
    charges, masses = charges[0, 0], masses[0, 0]
    places, atoms = charges.shape
    depth = places * PZ
    strips = lax.axis_size("grp")
    slots = task_first.shape[2]
    terms = kernel_taps.shape[0]
    rows = 4 * places
    number_far = strips - 3
    shape = jax.ShapeDtypeStruct
    vm = pltpu.VMEM
    dma = pltpu.SemaphoreType.DMA

    inputs = tuple(
        pltpu.with_memory_space_constraint(x, pltpu.HBM)
        for x in (cells, offsets, charges, task_first[0], task_second[0], kernel_taps)
    )
    pack = shape((2 * NE + rows + 8, 128), f32)
    store = vm((18 * places, atoms), f32)
    own, pk_lo, pk_hi, pos, lists, taps = call(
        functools.partial(spread_kernel, strips=strips),
        [shape((XO * YR, depth), f32), pack, pack, shape((rows, 128), f32)] + [shape((8, 128), f32)] * 2,
        [vm(x.shape, x.dtype) for x in inputs] + [vm((depth + 2 * PZ, 256), f32), dma((6,)), store],
        *inputs, task_count,
        hbm=range(6), smem=(6,),
    )
    up = shifted(pk_lo, "grp", -1)
    down = shifted(pk_hi, "grp", 1)
    far = [shifted(lists, "grp", d) for d in range(2, strips - 1)]

    force_shape = shape((3 * (places + 1) * 8, 128), f32)
    part_shape = shape((24 * (places + 1), 128), f32)
    pairs = [vm((128, 512), f32)] * UNROLL

    def sources(blocks):
        return vm((blocks * places * 8, 128), f32)

    table_shape = (2, XW * YR, terms * 256)
    line, edge_table, partial, force, parts = call(
        tables_kernel,
        [
            shape((2, terms, depth, depth), bf16),
            shape(table_shape, bf16),
            shape((XW * YR, depth), f32),
            force_shape,
            part_shape,
        ],
        [vm(table_shape, bf16), vm((2, terms * 256, depth), bf16), sources(1), *pairs],
        taps, own, pos,
        flops=10**10,
    )

    tables = -(-strips * slots // 128)
    column = call(
        functools.partial(column_kernel, number_far=number_far, strips=strips, slots=slots),
        [shape((3 * rows + 8 * tables, 128), f32)],
        [],
        up, down, pos, lists, *far,
    )[0]
    above = shifted(column, "patch", -1)
    below = shifted(column, "patch", 1)

    up, column = lax.optimization_barrier((up, column))
    pack = shape((2 * NS, 128), f32)
    edge = shape((2 * N2, 128), f32)
    to_low, to_high, edge_low, edge_high, mid = call(
        planes_kernel,
        [pack, pack, edge, edge, shape((XO * YR, depth), f32)],
        [vm((2, terms * 256, depth), bf16)],
        up, down, line, edge_table, partial,
    )
    high = shifted(to_low, "patch", -1)
    low = shifted(to_high, "patch", 1)
    e_hi = shifted(edge_low, "patch", -2)
    e_lo = shifted(edge_high, "patch", 2)

    work = (8, 2 * 128 * tables + 128)
    force, work_near = call(
        functools.partial(near_kernel, strips=strips),
        [force_shape, shape(work, i32)],
        [pltpu.SMEM(work, i32), sources(3), dma, *pairs],
        column, pos, force, parts,
        flops=10**10,
    )

    force, work_across = call(
        functools.partial(far_kernel, strips=strips, places=places),
        [force_shape, shape(work, i32)],
        [pltpu.SMEM(work, i32), sources(6), dma, *pairs],
        column, below, above, force, parts,
        flops=10**10,
    )
    half, moved = call(
        sample_kernel,
        [shape((3, places, atoms), f32), shape((3 * places, 128), f32)],
        [
            vm((3, places, atoms), f32),
            vm((XO * YR, depth), f32),
            vm((depth + 2 * PZ, XO * YR), f32),
            store,
        ],
        cells, offsets, charges, masses, velocity, pos, force, mid, low, high, e_lo, e_hi,
    )

    moved_up = shifted(moved, "grp", -1)
    moved_down = shifted(moved, "grp", 1)
    own_high = shifted(moved, "patch", -1)
    own_low = shifted(moved, "patch", 1)
    force, parts = call(
        moved_self_kernel,
        [force_shape, part_shape],
        [sources(1), *pairs],
        moved, pos,
        flops=10**10,
    )
    beside = jnp.concatenate([moved_down, moved_up], axis=0)
    moved_high = shifted(beside, "patch", -1)
    moved_low = shifted(beside, "patch", 1)
    force = call(
        moved_near_kernel,
        [force_shape],
        [sources(3), sources(6), *pairs],
        moved, moved_down, moved_up, own_low, own_high, column, below, above, force, parts, work_near, work_across,
        smem=(10, 11), flops=10**10,
    )[0]
    shown, speed = call(
        moved_far_kernel,
        [shape((3, places, atoms), f32)] * 2,
        [vm(force_shape.shape, f32), sources(6), *pairs],
        moved_low, moved_high, pos, below, above, force, parts, work_across, half, masses,
        smem=(7,),
    )
    return shown[:, None, None], speed[:, None, None]


def solution(mesh):
    placed = (
        P(None, "patch", "grp", None, None),
        P(None, "patch", "grp", None, None),
        P("patch", "grp", None, None),
        P("patch", "grp", None, None),
        P(None, "patch", "grp", None, None),
        P("patch", "grp", None),
        P("patch", "grp", None),
        P("patch", "grp"),
        P(),
    )
    return jax.shard_map(
        step,
        mesh=mesh,
        in_specs=placed,
        out_specs=(P(None, "patch", "grp", None, None), P(None, "patch", "grp", None, None)),
        check_vma=False,
    )
```

profile of v0, /device:TPU:3, one launch (start us, length us, event | category | flops | bytes accessed | tf_op | source)
XLA Modules:
  0.0 53.8 jit_solution(12327880355010979602)
XLA Ops:
  1.3 3.0 %shard_map.104 = (f32[240,256]{1,0:T(8,128)S(1)}, f32[344,128]{1,0:T(8,128)S(1)}, f32[344,128]{1,0:T(8,128)S(1)}, f32[128,128]{1,0:T(8,128)S(1)}, f32[8,128]{1,0:T(8,128)S(1)}, /*index=5*/f32[8,128]{1,0:T(8,128)S(1)}) custom-call(s32[3,32,128]{2,1,0:T(8,128)} %bitcast.13, f32[3,32,128]{2,1,0:T(8,128)} %bitcast.15, f32[32,128]{1,0:T(8,128)} %bitcast.19, ...), custom_call_target="tpu_custom_call" | custom-call | bytes 1048576 | tf_op jit(solution)/shard_map/pallas_call | solution.py:670
  4.3 3.4 %collective-permute-start = (f32[344,128]{1,0:T(8,128)S(1)}, f32[344,128]{1,0:T(8,128)S(1)}, u32[]{:S(2)}, u32[]{:S(2)}) collective-permute-start(f32[344,128]{1,0:T(8,128)S(1)} %get-tuple-element.31), channel_id=1, source_target_pairs={{0,3},{1,0},{2,1},{3,2},{4,7},{5,4},{6,5},{7,6},{8,11},{9,8},{10,9... | collective-permute-start | bytes 528392 | tf_op jit(solution)/shard_map/ppermute | solution.py:683
  7.7 0.0 collective-permute-start.1
  7.7 0.5 collective-permute-start.2
  8.1 5.6 %shard_map.106 = (bf16[2,6,256,256]{3,2,1,0:T(8,128)(2,1)S(1)}, bf16[2,624,1536]{2,1,0:T(8,128)(2,1)S(1)}, f32[624,256]{1,0:T(8,128)S(1)}, f32[792,128]{1,0:T(8,128)S(1)}, f32[792,128]{1,0:T(8,128)S(1)}) custom-call(f32[8,128]{1,0:T(8,128)S(1)} %get-tuple-element.35.taps, f32[240,256]{1,0:T(8,128)S(1)} %get-tuple-element.36.own, ...), custom_call_target="tpu_custom_call" | custom-call | flops 10000000000 | bytes 1048576 | tf_op jit(solution)/shard_map/pallas_call | solution.py:670
  13.8 1.0 %collective-permute-done.2.refs_4_ = f32[8,128]{1,0:T(8,128)S(1)} collective-permute-done((f32[8,128]{1,0:T(8,128)S(1)}, f32[8,128]{1,0:T(8,128)S(1)}, u32[]{:S(2)}, u32[]{:S(2)}) %collective-permute-start.2) | collective-permute-done | bytes 4128 | tf_op jit(solution)/shard_map/ppermute | solution.py:683
  14.8 0.0 collective-permute-done.refs_0_.up
  14.8 1.1 %collective-permute-done.1.refs_1_.down = f32[344,128]{1,0:T(8,128)S(1)} collective-permute-done((f32[344,128]{1,0:T(8,128)S(1)}, f32[344,128]{1,0:T(8,128)S(1)}, u32[]{:S(2)}, u32[]{:S(2)}) %collective-permute-start.1) | collective-permute-done | bytes 176160 | tf_op jit(solution)/shard_map/ppermute | solution.py:683
  15.9 0.1 shard_map.105.column.charged
  16.0 2.3 %collective-permute-start.3 = (f32[392,128]{1,0:T(8,128)S(1)}, f32[392,128]{1,0:T(8,128)S(1)}, u32[]{:S(2)}, u32[]{:S(2)}) collective-permute-start(f32[392,128]{1,0:T(8,128)S(1)} %shard_map.105.column.charged), channel_id=1, source_target_pairs={{0,4},{4,8},{8,12},{12,16},{16,20},{20,24},{24,28},{28,0},{1,5},{5... | collective-permute-start | bytes 602120 | tf_op jit(solution)/shard_map/ppermute | solution.py:683
  18.2 0.0 collective-permute-start.4
  18.2 2.2 %shard_map.109 = (f32[368,128]{1,0:T(8,128)S(1)}, f32[368,128]{1,0:T(8,128)S(1)}, f32[80,128]{1,0:T(8,128)S(1)}, f32[80,128]{1,0:T(8,128)S(1)}, f32[240,256]{1,0:T(8,128)S(1)}) custom-call(f32[344,128]{1,0:T(8,128)S(1)} %collective-permute-done.refs_0_.up, f32[344,128]{1,0:T(8,128)S(1)} %collective-permute-done.1.refs_1_.down, ...), custom_call_target="tpu_custom_call" | custom-call | bytes 1048576 | tf_op jit(solution)/shard_map/pallas_call | solution.py:670
  20.4 2.7 %collective-permute-start.5 = (f32[368,128]{1,0:T(8,128)S(1)}, f32[368,128]{1,0:T(8,128)S(1)}, u32[]{:S(2)}, u32[]{:S(2)}) collective-permute-start(f32[368,128]{1,0:T(8,128)S(1)} %get-tuple-element.46), channel_id=1, source_target_pairs={{0,4},{4,8},{8,12},{12,16},{16,20},{20,24},{24,28},{28,0},{1,5},{5... | collective-permute-start | bytes 565256 | tf_op jit(solution)/shard_map/ppermute | solution.py:683
  23.1 0.0 collective-permute-start.6
  23.1 0.3 collective-permute-start.7
  23.4 2.3 %shard_map.107 = (f32[792,128]{1,0:T(8,128)S(1)}, s32[8,384]{1,0:T(8,128)S(1)}) custom-call(f32[392,128]{1,0:T(8,128)S(1)} %shard_map.105.column.charged, f32[128,128]{1,0:T(8,128)S(1)} %get-tuple-element.30.refs_2_.pos, f32[792,128]{1,0:T(8,128)S(1)} %get-tuple-element.37.force_in, f32[792,128]{1,0:T(8,128)S(1)} %get-tuple-element.38.parts), custom_call_target="tpu_custom_call" | custom-call | flops 10000000000 | bytes 1048576 | tf_op jit(solution)/shard_map/pallas_call | solution.py:670
  25.7 0.0 collective-permute-done.3.below
  25.7 1.2 %collective-permute-start.8 = (f32[80,128]{1,0:T(8,128)S(1)}, f32[80,128]{1,0:T(8,128)S(1)}, u32[]{:S(2)}, u32[]{:S(2)}) collective-permute-start(f32[80,128]{1,0:T(8,128)S(1)} %get-tuple-element.49), channel_id=1, source_target_pairs={{0,24},{4,28},{8,0},{12,4},{16,8},{20,12},{24,16},{28,20},{1,25},{... | collective-permute-start | bytes 122888 | tf_op jit(solution)/shard_map/ppermute | solution.py:683
  27.0 0.0 collective-permute-done.4.above
  27.0 0.0 copy-start
  27.0 0.0 copy-start.3
  27.0 0.0 copy-start.4
  27.0 2.9 %shard_map.108 = (f32[792,128]{1,0:T(8,128)S(1)}, s32[8,384]{1,0:T(8,128)S(1)}) custom-call(f32[392,128]{1,0:T(8,128)S(1)} %shard_map.105.column.charged, f32[392,128]{1,0:T(8,128)S(1)} %collective-permute-done.3.below, f32[392,128]{1,0:T(8,128)S(1)} %collective-permute-done.4.above, f32[792,128]{1,0:T(8,128)S(1)} %get-tuple-element.39.force_in, ...), custom_call_target="tpu_custom_call" | custom-call | flops 10000000000 | bytes 1048576 | tf_op jit(solution)/shard_map/pallas_call | solution.py:670
  29.9 0.0 collective-permute-done.7.e_lo
  29.9 0.1 collective-permute-done.8.e_hi
  30.0 0.0 collective-permute-done.5.low
  30.0 0.0 collective-permute-done.6.high
  30.0 0.0 copy-done
  30.0 0.0 copy-done.1
  30.0 0.0 copy-done.2
  30.0 0.0 copy-done.3
  30.0 0.0 copy-done.4
  30.0 2.4 %shard_map.110 = (f32[3,32,128]{2,1,0:T(8,128)S(1)}, f32[96,128]{1,0:T(8,128)S(1)}) custom-call(s32[3,32,128]{2,1,0:T(8,128)S(1)} %bitcast.14, f32[3,32,128]{2,1,0:T(8,128)S(1)} %bitcast.16, f32[32,128]{1,0:T(8,128)S(1)} %bitcast.20, f32[32,128]{1,0:T(8,128)S(1)} %bitcast.17, f32[3,32,128]{2,1,0:T(8,128)S(1)} %bitcast.21, ...), custom_call_target="tpu_custom_call" | custom-call | bytes 1048576 | tf_op jit(solution)/shard_map/pallas_call | solution.py:670
  32.4 1.4 %collective-permute-start.9 = (f32[96,128]{1,0:T(8,128)S(1)}, f32[96,128]{1,0:T(8,128)S(1)}, u32[]{:S(2)}, u32[]{:S(2)}) collective-permute-start(f32[96,128]{1,0:T(8,128)S(1)} %get-tuple-element.50.moved), channel_id=1, source_target_pairs={{0,1},{1,2},{2,3},{3,0},{4,5},{5,6},{6,7},{7,4},{8,9},{9,10},{10,1... | collective-permute-start | bytes 147464 | tf_op jit(solution)/shard_map/ppermute | solution.py:683
  33.8 2.4 %shard_map.111 = (f32[792,128]{1,0:T(8,128)S(1)}, f32[792,128]{1,0:T(8,128)S(1)}) custom-call(f32[96,128]{1,0:T(8,128)S(1)} %get-tuple-element.50.moved, f32[128,128]{1,0:T(8,128)S(1)} %get-tuple-element.30.refs_2_.pos), custom_call_target="tpu_custom_call" | custom-call | flops 10000000000 | bytes 1048576 | tf_op jit(solution)/shard_map/pallas_call | solution.py:670
  36.2 2.0 %collective-permute-start.10 = (f32[96,128]{1,0:T(8,128)S(1)}, f32[96,128]{1,0:T(8,128)S(1)}, u32[]{:S(2)}, u32[]{:S(2)}) collective-permute-start(f32[96,128]{1,0:T(8,128)S(1)} %get-tuple-element.50.moved), channel_id=1, source_target_pairs={{0,3},{1,0},{2,1},{3,2},{4,7},{5,4},{6,5},{7,6},{8,11},{9,8},{10,9... | collective-permute-start | bytes 147464 | tf_op jit(solution)/shard_map/ppermute | solution.py:683
  38.2 4.6 %collective-permute-start.13 = (f32[96,128]{1,0:T(8,128)S(1)}, f32[96,128]{1,0:T(8,128)S(1)}, u32[]{:S(2)}, u32[]{:S(2)}) collective-permute-start(f32[96,128]{1,0:T(8,128)S(1)} %get-tuple-element.50.moved), channel_id=1, source_target_pairs={{0,4},{4,8},{8,12},{12,16},{16,20},{20,24},{24,28},{28,0},{1,5},{5... | collective-permute-start | bytes 147464 | tf_op jit(solution)/shard_map/ppermute | solution.py:683
  42.8 0.0 collective-permute-start.14
  42.8 0.0 collective-permute-done.9.below_strip
  42.8 0.0 collective-permute-done.10.above_strip
  42.8 2.7 %collective-permute-start.11 = (f32[192,128]{1,0:T(8,128)S(1)}, f32[192,128]{1,0:T(8,128)S(1)}, u32[]{:S(2)}, u32[]{:S(2)}) collective-permute-start(f32[192,128]{1,0:T(8,128)S(1)} %constant_dynamic-update-slice_fusion), channel_id=1, source_target_pairs={{0,4},{4,8},{8,12},{12,16},{16,20},{20,24},{24,28},{28,0},{1,5},{5... | collective-permute-start | bytes 294920 | tf_op jit(solution)/shard_map/ppermute | solution.py:683
  45.5 0.0 collective-permute-start.12
  45.5 0.0 collective-permute-done.13.low
  45.5 2.2 %collective-permute-done.14.high = f32[96,128]{1,0:T(8,128)S(1)} collective-permute-done((f32[96,128]{1,0:T(8,128)S(1)}, f32[96,128]{1,0:T(8,128)S(1)}, u32[]{:S(2)}, u32[]{:S(2)}) %collective-permute-start.14) | collective-permute-done | bytes 49184 | tf_op jit(solution)/shard_map/ppermute | solution.py:683
  47.7 2.8 %shard_map.112.force_in = f32[792,128]{1,0:T(8,128)S(1)} custom-call(f32[96,128]{1,0:T(8,128)S(1)} %get-tuple-element.50.moved, f32[96,128]{1,0:T(8,128)S(1)} %collective-permute-done.9.below_strip, f32[96,128]{1,0:T(8,128)S(1)} %collective-permute-done.10.above_strip, f32[96,128]{1,0:T(8,128)S(1)} %collective-permute-done.13.low, ...), custom_call_target="tpu_custom_call" | custom-call | flops 10000000000 | bytes 1048576 | tf_op jit(solution)/shard_map/pallas_call | solution.py:670
  50.5 0.0 collective-permute-done.11.low
  50.5 0.0 collective-permute-done.12.high
  50.5 3.3 %shard_map.113 = (f32[3,32,128]{2,1,0:T(8,128)}, f32[3,32,128]{2,1,0:T(8,128)}) custom-call(f32[192,128]{1,0:T(8,128)S(1)} %collective-permute-done.11.low, f32[192,128]{1,0:T(8,128)S(1)} %collective-permute-done.12.high, f32[128,128]{1,0:T(8,128)S(1)} %get-tuple-element.30.refs_2_.pos, f32[392,128]{1,0:T(8,128)S(1)} %collective-permute-done.3.below, ...), custom_call_target="tpu_custom_call" | custom-call | bytes 1048576 | tf_op jit(solution)/shard_map/pallas_call | solution.py:670
  (4 shorter events, 0.0 us)
Async XLA Ops:
  4.3 10.5 %collective-permute-start = (f32[344,128]{1,0:T(8,128)S(1)}, f32[344,128]{1,0:T(8,128)S(1)}, u32[]{:S(2)}, u32[]{:S(2)}) collective-permute-start(f32[344,128]{1,0:T(8,128)S(1)} %get-tuple-element.31), channel_id=1, source_target_pairs={{0,3},{1,0},{2,1},{3,2},{4,7},{5,4},{6,5},{7,6},{8,11},{9,8},{10,9... | collective-permute-start | bytes 528392 | tf_op jit(solution)/shard_map/ppermute | solution.py:683
  7.7 8.2 %collective-permute-start.1 = (f32[344,128]{1,0:T(8,128)S(1)}, f32[344,128]{1,0:T(8,128)S(1)}, u32[]{:S(2)}, u32[]{:S(2)}) collective-permute-start(f32[344,128]{1,0:T(8,128)S(1)} %get-tuple-element.32), channel_id=1, source_target_pairs={{0,1},{1,2},{2,3},{3,0},{4,5},{5,6},{6,7},{7,4},{8,9},{9,10},{10,1... | collective-permute-start | bytes 528392 | tf_op jit(solution)/shard_map/ppermute | solution.py:683
  7.7 7.1 %collective-permute-start.2 = (f32[8,128]{1,0:T(8,128)S(1)}, f32[8,128]{1,0:T(8,128)S(1)}, u32[]{:S(2)}, u32[]{:S(2)}) collective-permute-start(f32[8,128]{1,0:T(8,128)S(1)} %get-tuple-element.33.refs_3_), channel_id=1, source_target_pairs={{0,2},{1,3},{2,0},{3,1},{4,6},{5,7},{6,4},{7,5},{8,10},{9,11},{10,... | collective-permute-start | bytes 12296 | tf_op jit(solution)/shard_map/ppermute | solution.py:683
  16.0 9.8 %collective-permute-start.3 = (f32[392,128]{1,0:T(8,128)S(1)}, f32[392,128]{1,0:T(8,128)S(1)}, u32[]{:S(2)}, u32[]{:S(2)}) collective-permute-start(f32[392,128]{1,0:T(8,128)S(1)} %shard_map.105.column.charged), channel_id=1, source_target_pairs={{0,4},{4,8},{8,12},{12,16},{16,20},{20,24},{24,28},{28,0},{1,5},{5... | collective-permute-start | bytes 602120 | tf_op jit(solution)/shard_map/ppermute | solution.py:683
  18.2 8.7 %collective-permute-start.4 = (f32[392,128]{1,0:T(8,128)S(1)}, f32[392,128]{1,0:T(8,128)S(1)}, u32[]{:S(2)}, u32[]{:S(2)}) collective-permute-start(f32[392,128]{1,0:T(8,128)S(1)} %shard_map.105.column.charged), channel_id=1, source_target_pairs={{0,28},{4,0},{8,4},{12,8},{16,12},{20,16},{24,20},{28,24},{1,29},{... | collective-permute-start | bytes 602120 | tf_op jit(solution)/shard_map/ppermute | solution.py:683
  20.4 9.6 %collective-permute-start.5 = (f32[368,128]{1,0:T(8,128)S(1)}, f32[368,128]{1,0:T(8,128)S(1)}, u32[]{:S(2)}, u32[]{:S(2)}) collective-permute-start(f32[368,128]{1,0:T(8,128)S(1)} %get-tuple-element.46), channel_id=1, source_target_pairs={{0,4},{4,8},{8,12},{12,16},{16,20},{20,24},{24,28},{28,0},{1,5},{5... | collective-permute-start | bytes 565256 | tf_op jit(solution)/shard_map/ppermute | solution.py:683
  23.1 6.9 %collective-permute-start.6 = (f32[368,128]{1,0:T(8,128)S(1)}, f32[368,128]{1,0:T(8,128)S(1)}, u32[]{:S(2)}, u32[]{:S(2)}) collective-permute-start(f32[368,128]{1,0:T(8,128)S(1)} %get-tuple-element.47), channel_id=1, source_target_pairs={{0,28},{4,0},{8,4},{12,8},{16,12},{20,16},{24,20},{28,24},{1,29},{... | collective-permute-start | bytes 565256 | tf_op jit(solution)/shard_map/ppermute | solution.py:683
  23.1 6.7 %collective-permute-start.7 = (f32[80,128]{1,0:T(8,128)S(1)}, f32[80,128]{1,0:T(8,128)S(1)}, u32[]{:S(2)}, u32[]{:S(2)}) collective-permute-start(f32[80,128]{1,0:T(8,128)S(1)} %get-tuple-element.48), channel_id=1, source_target_pairs={{0,8},{4,12},{8,16},{12,20},{16,24},{20,28},{24,0},{28,4},{1,9},{5... | collective-permute-start | bytes 122888 | tf_op jit(solution)/shard_map/ppermute | solution.py:683
  25.7 4.2 %collective-permute-start.8 = (f32[80,128]{1,0:T(8,128)S(1)}, f32[80,128]{1,0:T(8,128)S(1)}, u32[]{:S(2)}, u32[]{:S(2)}) collective-permute-start(f32[80,128]{1,0:T(8,128)S(1)} %get-tuple-element.49), channel_id=1, source_target_pairs={{0,24},{4,28},{8,0},{12,4},{16,8},{20,12},{24,16},{28,20},{1,25},{... | collective-permute-start | bytes 122888 | tf_op jit(solution)/shard_map/ppermute | solution.py:683
  27.0 3.0 %copy-start = (s32[3,1,1,32,128]{4,3,2,1,0:T(8,128)S(1)}, s32[3,1,1,32,128]{4,3,2,1,0:T(8,128)}, u32[]{:S(2)}) copy-start(s32[3,1,1,32,128]{4,3,2,1,0:T(8,128)} %param.9) | copy-start | bytes 147460
  27.0 3.0 %copy-start.1 = (f32[3,1,1,32,128]{4,3,2,1,0:T(8,128)S(1)}, f32[3,1,1,32,128]{4,3,2,1,0:T(8,128)}, u32[]{:S(2)}) copy-start(f32[3,1,1,32,128]{4,3,2,1,0:T(8,128)} %param.10) | copy-start | bytes 147460
  27.0 3.1 %copy-start.2 = (f32[1,1,32,128]{3,2,1,0:T(8,128)S(1)}, f32[1,1,32,128]{3,2,1,0:T(8,128)}, u32[]{:S(2)}) copy-start(f32[1,1,32,128]{3,2,1,0:T(8,128)} %param.12) | copy-start | bytes 49156
  27.0 3.1 %copy-start.3 = (f32[1,1,32,128]{3,2,1,0:T(8,128)S(1)}, f32[1,1,32,128]{3,2,1,0:T(8,128)}, u32[]{:S(2)}) copy-start(f32[1,1,32,128]{3,2,1,0:T(8,128)} %param.11) | copy-start | bytes 49156
  27.0 3.1 %copy-start.4 = (f32[3,1,1,32,128]{4,3,2,1,0:T(8,128)S(1)}, f32[3,1,1,32,128]{4,3,2,1,0:T(8,128)}, u32[]{:S(2)}) copy-start(f32[3,1,1,32,128]{4,3,2,1,0:T(8,128)} %param.13) | copy-start | bytes 147460
  32.4 10.4 %collective-permute-start.9 = (f32[96,128]{1,0:T(8,128)S(1)}, f32[96,128]{1,0:T(8,128)S(1)}, u32[]{:S(2)}, u32[]{:S(2)}) collective-permute-start(f32[96,128]{1,0:T(8,128)S(1)} %get-tuple-element.50.moved), channel_id=1, source_target_pairs={{0,1},{1,2},{2,3},{3,0},{4,5},{5,6},{6,7},{7,4},{8,9},{9,10},{10,1... | collective-permute-start | bytes 147464 | tf_op jit(solution)/shard_map/ppermute | solution.py:683
  36.2 6.6 %collective-permute-start.10 = (f32[96,128]{1,0:T(8,128)S(1)}, f32[96,128]{1,0:T(8,128)S(1)}, u32[]{:S(2)}, u32[]{:S(2)}) collective-permute-start(f32[96,128]{1,0:T(8,128)S(1)} %get-tuple-element.50.moved), channel_id=1, source_target_pairs={{0,3},{1,0},{2,1},{3,2},{4,7},{5,4},{6,5},{7,6},{8,11},{9,8},{10,9... | collective-permute-start | bytes 147464 | tf_op jit(solution)/shard_map/ppermute | solution.py:683
  38.2 7.3 %collective-permute-start.13 = (f32[96,128]{1,0:T(8,128)S(1)}, f32[96,128]{1,0:T(8,128)S(1)}, u32[]{:S(2)}, u32[]{:S(2)}) collective-permute-start(f32[96,128]{1,0:T(8,128)S(1)} %get-tuple-element.50.moved), channel_id=1, source_target_pairs={{0,4},{4,8},{8,12},{12,16},{16,20},{20,24},{24,28},{28,0},{1,5},{5... | collective-permute-start | bytes 147464 | tf_op jit(solution)/shard_map/ppermute | solution.py:683
  42.8 4.9 %collective-permute-start.14 = (f32[96,128]{1,0:T(8,128)S(1)}, f32[96,128]{1,0:T(8,128)S(1)}, u32[]{:S(2)}, u32[]{:S(2)}) collective-permute-start(f32[96,128]{1,0:T(8,128)S(1)} %get-tuple-element.50.moved), channel_id=1, source_target_pairs={{0,28},{4,0},{8,4},{12,8},{16,12},{20,16},{24,20},{28,24},{1,29},{... | collective-permute-start | bytes 147464 | tf_op jit(solution)/shard_map/ppermute | solution.py:683
  42.8 7.7 %collective-permute-start.11 = (f32[192,128]{1,0:T(8,128)S(1)}, f32[192,128]{1,0:T(8,128)S(1)}, u32[]{:S(2)}, u32[]{:S(2)}) collective-permute-start(f32[192,128]{1,0:T(8,128)S(1)} %constant_dynamic-update-slice_fusion), channel_id=1, source_target_pairs={{0,4},{4,8},{8,12},{12,16},{16,20},{20,24},{24,28},{28,0},{1,5},{5... | collective-permute-start | bytes 294920 | tf_op jit(solution)/shard_map/ppermute | solution.py:683
  45.5 5.0 %collective-permute-start.12 = (f32[192,128]{1,0:T(8,128)S(1)}, f32[192,128]{1,0:T(8,128)S(1)}, u32[]{:S(2)}, u32[]{:S(2)}) collective-permute-start(f32[192,128]{1,0:T(8,128)S(1)} %constant_dynamic-update-slice_fusion), channel_id=1, source_target_pairs={{0,28},{4,0},{8,4},{12,8},{16,12},{20,16},{24,20},{28,24},{1,29},{... | collective-permute-start | bytes 294920 | tf_op jit(solution)/shard_map/ppermute | solution.py:683
where the time goes:
time: 54 us; the launch traced here: 53.8 us
  Pallas kernels  26.9 us (50%)
  starting transfers between devices  20.9 us (39%)
  waiting for transfers between devices  4.48 us (8%)
  between operations  1.46 us (3%)
    pallas_call x10, Pallas kernels, call(): pl.pallas_call(kernel, out_shape=outs, in_specs=[pl.BlockSpec(memory_spac...  26.9 us
    ppermute x15, starting transfers between devices, shifted(): lax.ppermute(x, axis, [(i, (i + distance) % size) for i in range(size)])  20.9 us
    ppermute x15, waiting for transfers between devices, shifted(): lax.ppermute(x, axis, [(i, (i + distance) % size) for i in range(size)])  4.48 us
  transfers between devices with their start and end apart: 15, of which 4 were waited for; matrix products, arithmetic and copies ran while one was open for 0% of the time, Pallas kernels for 34%

commit v1 on v0

--- a/solution.py
+++ b/solution.py
@@ -255,14 +255,14 @@
         return jnp.where(n < number, decode(n)[0], places)
 
     def body(m, carry):
-        n = UNROLL * m
+        n = len(pairs) * m
         for u, dst in enumerate(pairs):
             prepare(n + u, dst)
         for u, dst in enumerate(pairs):
             side_push(force, dst, receiver(n + u))
         return carry
 
-    lax.fori_loop(0, (number + UNROLL - 1) // UNROLL, body, 0)
+    lax.fori_loop(0, (number + len(pairs) - 1) // len(pairs), body, 0)
 
 
 def fill_sources(src, block, component, places):
@@ -733,7 +733,7 @@
             force_shape,
             part_shape,
         ],
-        [vm(table_shape, bf16), vm((2, terms * 256, depth), bf16), sources(1), *pairs],
+        [vm(table_shape, bf16), vm((2, terms * 256, depth), bf16), sources(1), *pairs, *pairs],
         taps, own, pos,
         flops=10**10,
     )
@@ -797,7 +797,7 @@
     force, parts = call(
         moved_self_kernel,
         [force_shape, part_shape],
-        [sources(1), *pairs],
+        [sources(1), *pairs, *pairs],
         moved, pos,
         flops=10**10,
     )

time: 54 us -> 53.8 us (level)
  Pallas kernels: 26.9 us -> 26.1 us
    pallas_call x10, Pallas kernels: 26.9 us -> 26.1 us  [call(): pl.pallas_call(kernel, out_shape=outs, in_specs=[pl.BlockSpec(memory_spac...]
  transfers between devices with their start and end apart: 15 -> 15, of which waited for: 4 -> 4; matrix products, arithmetic and copies ran while one was open for 0% -> 0% of each run, Pallas kernels for 34% -> 32%
where the time goes in v1:
time: 53.8 us; the launch traced here: 53.6 us
  Pallas kernels  26.1 us (49%)
  starting transfers between devices  21.1 us (39%)
  waiting for transfers between devices  4.86 us (9%)
  between operations  1.46 us (3%)
    pallas_call x10, Pallas kernels, call(): pl.pallas_call(kernel, out_shape=outs, in_specs=[pl.BlockSpec(memory_spac...  26.1 us
    ppermute x15, starting transfers between devices, shifted(): lax.ppermute(x, axis, [(i, (i + distance) % size) for i in range(size)])  21.1 us
    ppermute x15, waiting for transfers between devices, shifted(): lax.ppermute(x, axis, [(i, (i + distance) % size) for i in range(size)])  4.86 us
  transfers between devices with their start and end apart: 15, of which 4 were waited for; matrix products, arithmetic and copies ran while one was open for 0% of the time, Pallas kernels for 32%

profile of v1, /device:TPU:3, one launch (start us, length us, event | category | flops | bytes accessed | tf_op | source)
XLA Modules:
  0.0 53.6 jit_solution(5286679291132902283)
XLA Ops:
  1.3 3.0 %shard_map.104 = (f32[240,256]{1,0:T(8,128)S(1)}, f32[344,128]{1,0:T(8,128)S(1)}, f32[344,128]{1,0:T(8,128)S(1)}, f32[128,128]{1,0:T(8,128)S(1)}, f32[8,128]{1,0:T(8,128)S(1)}, /*index=5*/f32[8,128]{1,0:T(8,128)S(1)}) custom-call(s32[3,32,128]{2,1,0:T(8,128)} %bitcast.13, f32[3,32,128]{2,1,0:T(8,128)} %bitcast.15, f32[32,128]{1,0:T(8,128)} %bitcast.19, ...), custom_call_target="tpu_custom_call" | custom-call | bytes 1048576 | tf_op jit(solution)/shard_map/pallas_call | solution.py:670
  4.3 3.4 %collective-permute-start = (f32[344,128]{1,0:T(8,128)S(1)}, f32[344,128]{1,0:T(8,128)S(1)}, u32[]{:S(2)}, u32[]{:S(2)}) collective-permute-start(f32[344,128]{1,0:T(8,128)S(1)} %get-tuple-element.31), channel_id=1, source_target_pairs={{0,3},{1,0},{2,1},{3,2},{4,7},{5,4},{6,5},{7,6},{8,11},{9,8},{10,9... | collective-permute-start | bytes 528392 | tf_op jit(solution)/shard_map/ppermute | solution.py:683
  7.7 0.0 collective-permute-start.1
  7.7 0.4 collective-permute-start.2
  8.1 5.2 %shard_map.106 = (bf16[2,6,256,256]{3,2,1,0:T(8,128)(2,1)S(1)}, bf16[2,624,1536]{2,1,0:T(8,128)(2,1)S(1)}, f32[624,256]{1,0:T(8,128)S(1)}, f32[792,128]{1,0:T(8,128)S(1)}, f32[792,128]{1,0:T(8,128)S(1)}) custom-call(f32[8,128]{1,0:T(8,128)S(1)} %get-tuple-element.35.taps, f32[240,256]{1,0:T(8,128)S(1)} %get-tuple-element.36.own, ...), custom_call_target="tpu_custom_call" | custom-call | flops 10000000000 | bytes 1048576 | tf_op jit(solution)/shard_map/pallas_call | solution.py:670
  13.4 1.4 %collective-permute-done.2.refs_4_ = f32[8,128]{1,0:T(8,128)S(1)} collective-permute-done((f32[8,128]{1,0:T(8,128)S(1)}, f32[8,128]{1,0:T(8,128)S(1)}, u32[]{:S(2)}, u32[]{:S(2)}) %collective-permute-start.2) | collective-permute-done | bytes 4128 | tf_op jit(solution)/shard_map/ppermute | solution.py:683
  14.8 0.0 collective-permute-done.refs_0_.up
  14.8 1.1 %collective-permute-done.1.refs_1_.down = f32[344,128]{1,0:T(8,128)S(1)} collective-permute-done((f32[344,128]{1,0:T(8,128)S(1)}, f32[344,128]{1,0:T(8,128)S(1)}, u32[]{:S(2)}, u32[]{:S(2)}) %collective-permute-start.1) | collective-permute-done | bytes 176160 | tf_op jit(solution)/shard_map/ppermute | solution.py:683
  15.9 0.1 shard_map.105.column.charged
  16.0 2.3 %collective-permute-start.3 = (f32[392,128]{1,0:T(8,128)S(1)}, f32[392,128]{1,0:T(8,128)S(1)}, u32[]{:S(2)}, u32[]{:S(2)}) collective-permute-start(f32[392,128]{1,0:T(8,128)S(1)} %shard_map.105.column.charged), channel_id=1, source_target_pairs={{0,4},{4,8},{8,12},{12,16},{16,20},{20,24},{24,28},{28,0},{1,5},{5... | collective-permute-start | bytes 602120 | tf_op jit(solution)/shard_map/ppermute | solution.py:683
  18.2 0.0 collective-permute-start.4
  18.2 2.2 %shard_map.109 = (f32[368,128]{1,0:T(8,128)S(1)}, f32[368,128]{1,0:T(8,128)S(1)}, f32[80,128]{1,0:T(8,128)S(1)}, f32[80,128]{1,0:T(8,128)S(1)}, f32[240,256]{1,0:T(8,128)S(1)}) custom-call(f32[344,128]{1,0:T(8,128)S(1)} %collective-permute-done.refs_0_.up, f32[344,128]{1,0:T(8,128)S(1)} %collective-permute-done.1.refs_1_.down, ...), custom_call_target="tpu_custom_call" | custom-call | bytes 1048576 | tf_op jit(solution)/shard_map/pallas_call | solution.py:670
  20.4 2.7 %collective-permute-start.5 = (f32[368,128]{1,0:T(8,128)S(1)}, f32[368,128]{1,0:T(8,128)S(1)}, u32[]{:S(2)}, u32[]{:S(2)}) collective-permute-start(f32[368,128]{1,0:T(8,128)S(1)} %get-tuple-element.46), channel_id=1, source_target_pairs={{0,4},{4,8},{8,12},{12,16},{16,20},{20,24},{24,28},{28,0},{1,5},{5... | collective-permute-start | bytes 565256 | tf_op jit(solution)/shard_map/ppermute | solution.py:683
  23.1 0.0 collective-permute-start.6
  23.1 0.3 collective-permute-start.7
  23.4 2.3 %shard_map.107 = (f32[792,128]{1,0:T(8,128)S(1)}, s32[8,384]{1,0:T(8,128)S(1)}) custom-call(f32[392,128]{1,0:T(8,128)S(1)} %shard_map.105.column.charged, f32[128,128]{1,0:T(8,128)S(1)} %get-tuple-element.30.refs_2_.pos, f32[792,128]{1,0:T(8,128)S(1)} %get-tuple-element.37.force_in, f32[792,128]{1,0:T(8,128)S(1)} %get-tuple-element.38.parts), custom_call_target="tpu_custom_call" | custom-call | flops 10000000000 | bytes 1048576 | tf_op jit(solution)/shard_map/pallas_call | solution.py:670
  25.7 0.0 collective-permute-done.3.below
  25.7 1.2 %collective-permute-start.8 = (f32[80,128]{1,0:T(8,128)S(1)}, f32[80,128]{1,0:T(8,128)S(1)}, u32[]{:S(2)}, u32[]{:S(2)}) collective-permute-start(f32[80,128]{1,0:T(8,128)S(1)} %get-tuple-element.49), channel_id=1, source_target_pairs={{0,24},{4,28},{8,0},{12,4},{16,8},{20,12},{24,16},{28,20},{1,25},{... | collective-permute-start | bytes 122888 | tf_op jit(solution)/shard_map/ppermute | solution.py:683
  27.0 0.0 collective-permute-done.4.above
  27.0 0.0 copy-start
  27.0 0.0 copy-start.3
  27.0 0.0 copy-start.4
  27.0 2.9 %shard_map.108 = (f32[792,128]{1,0:T(8,128)S(1)}, s32[8,384]{1,0:T(8,128)S(1)}) custom-call(f32[392,128]{1,0:T(8,128)S(1)} %shard_map.105.column.charged, f32[392,128]{1,0:T(8,128)S(1)} %collective-permute-done.3.below, f32[392,128]{1,0:T(8,128)S(1)} %collective-permute-done.4.above, f32[792,128]{1,0:T(8,128)S(1)} %get-tuple-element.39.force_in, ...), custom_call_target="tpu_custom_call" | custom-call | flops 10000000000 | bytes 1048576 | tf_op jit(solution)/shard_map/pallas_call | solution.py:670
  29.9 0.0 collective-permute-done.7.e_lo
  29.9 0.1 collective-permute-done.8.e_hi
  30.0 0.0 collective-permute-done.5.low
  30.0 0.0 collective-permute-done.6.high
  30.0 0.0 copy-done
  30.0 0.0 copy-done.1
  30.0 0.0 copy-done.2
  30.0 0.0 copy-done.3
  30.0 0.0 copy-done.4
  30.0 2.4 %shard_map.110 = (f32[3,32,128]{2,1,0:T(8,128)S(1)}, f32[96,128]{1,0:T(8,128)S(1)}) custom-call(s32[3,32,128]{2,1,0:T(8,128)S(1)} %bitcast.14, f32[3,32,128]{2,1,0:T(8,128)S(1)} %bitcast.16, f32[32,128]{1,0:T(8,128)S(1)} %bitcast.20, f32[32,128]{1,0:T(8,128)S(1)} %bitcast.17, f32[3,32,128]{2,1,0:T(8,128)S(1)} %bitcast.21, ...), custom_call_target="tpu_custom_call" | custom-call | bytes 1048576 | tf_op jit(solution)/shard_map/pallas_call | solution.py:670
  32.4 1.6 %collective-permute-start.9 = (f32[96,128]{1,0:T(8,128)S(1)}, f32[96,128]{1,0:T(8,128)S(1)}, u32[]{:S(2)}, u32[]{:S(2)}) collective-permute-start(f32[96,128]{1,0:T(8,128)S(1)} %get-tuple-element.50.moved), channel_id=1, source_target_pairs={{0,1},{1,2},{2,3},{3,0},{4,5},{5,6},{6,7},{7,4},{8,9},{9,10},{10,1... | collective-permute-start | bytes 147464 | tf_op jit(solution)/shard_map/ppermute | solution.py:683
  34.0 2.0 %shard_map.111 = (f32[792,128]{1,0:T(8,128)S(1)}, f32[792,128]{1,0:T(8,128)S(1)}) custom-call(f32[96,128]{1,0:T(8,128)S(1)} %get-tuple-element.50.moved, f32[128,128]{1,0:T(8,128)S(1)} %get-tuple-element.30.refs_2_.pos), custom_call_target="tpu_custom_call" | custom-call | flops 10000000000 | bytes 1048576 | tf_op jit(solution)/shard_map/pallas_call | solution.py:670
  36.0 2.0 %collective-permute-start.10 = (f32[96,128]{1,0:T(8,128)S(1)}, f32[96,128]{1,0:T(8,128)S(1)}, u32[]{:S(2)}, u32[]{:S(2)}) collective-permute-start(f32[96,128]{1,0:T(8,128)S(1)} %get-tuple-element.50.moved), channel_id=1, source_target_pairs={{0,3},{1,0},{2,1},{3,2},{4,7},{5,4},{6,5},{7,6},{8,11},{9,8},{10,9... | collective-permute-start | bytes 147464 | tf_op jit(solution)/shard_map/ppermute | solution.py:683
  38.0 4.6 %collective-permute-start.13 = (f32[96,128]{1,0:T(8,128)S(1)}, f32[96,128]{1,0:T(8,128)S(1)}, u32[]{:S(2)}, u32[]{:S(2)}) collective-permute-start(f32[96,128]{1,0:T(8,128)S(1)} %get-tuple-element.50.moved), channel_id=1, source_target_pairs={{0,4},{4,8},{8,12},{12,16},{16,20},{20,24},{24,28},{28,0},{1,5},{5... | collective-permute-start | bytes 147464 | tf_op jit(solution)/shard_map/ppermute | solution.py:683
  42.5 0.0 collective-permute-start.14
  42.5 0.0 collective-permute-done.9.below_strip
  42.5 0.0 collective-permute-done.10.above_strip
  42.6 2.7 %collective-permute-start.11 = (f32[192,128]{1,0:T(8,128)S(1)}, f32[192,128]{1,0:T(8,128)S(1)}, u32[]{:S(2)}, u32[]{:S(2)}) collective-permute-start(f32[192,128]{1,0:T(8,128)S(1)} %constant_dynamic-update-slice_fusion), channel_id=1, source_target_pairs={{0,4},{4,8},{8,12},{12,16},{16,20},{20,24},{24,28},{28,0},{1,5},{5... | collective-permute-start | bytes 294920 | tf_op jit(solution)/shard_map/ppermute | solution.py:683
  45.3 0.0 collective-permute-start.12
  45.3 0.0 collective-permute-done.13.low
  45.3 2.2 %collective-permute-done.14.high = f32[96,128]{1,0:T(8,128)S(1)} collective-permute-done((f32[96,128]{1,0:T(8,128)S(1)}, f32[96,128]{1,0:T(8,128)S(1)}, u32[]{:S(2)}, u32[]{:S(2)}) %collective-permute-start.14) | collective-permute-done | bytes 49184 | tf_op jit(solution)/shard_map/ppermute | solution.py:683
  47.5 2.8 %shard_map.112.force_in = f32[792,128]{1,0:T(8,128)S(1)} custom-call(f32[96,128]{1,0:T(8,128)S(1)} %get-tuple-element.50.moved, f32[96,128]{1,0:T(8,128)S(1)} %collective-permute-done.9.below_strip, f32[96,128]{1,0:T(8,128)S(1)} %collective-permute-done.10.above_strip, f32[96,128]{1,0:T(8,128)S(1)} %collective-permute-done.13.low, ...), custom_call_target="tpu_custom_call" | custom-call | flops 10000000000 | bytes 1048576 | tf_op jit(solution)/shard_map/pallas_call | solution.py:670
  50.2 0.0 collective-permute-done.11.low
  50.2 0.0 collective-permute-done.12.high
  50.3 3.3 %shard_map.113 = (f32[3,32,128]{2,1,0:T(8,128)}, f32[3,32,128]{2,1,0:T(8,128)}) custom-call(f32[192,128]{1,0:T(8,128)S(1)} %collective-permute-done.11.low, f32[192,128]{1,0:T(8,128)S(1)} %collective-permute-done.12.high, f32[128,128]{1,0:T(8,128)S(1)} %get-tuple-element.30.refs_2_.pos, f32[392,128]{1,0:T(8,128)S(1)} %collective-permute-done.3.below, ...), custom_call_target="tpu_custom_call" | custom-call | bytes 1048576 | tf_op jit(solution)/shard_map/pallas_call | solution.py:670
  (4 shorter events, 0.0 us)
Async XLA Ops:
  4.3 10.5 %collective-permute-start = (f32[344,128]{1,0:T(8,128)S(1)}, f32[344,128]{1,0:T(8,128)S(1)}, u32[]{:S(2)}, u32[]{:S(2)}) collective-permute-start(f32[344,128]{1,0:T(8,128)S(1)} %get-tuple-element.31), channel_id=1, source_target_pairs={{0,3},{1,0},{2,1},{3,2},{4,7},{5,4},{6,5},{7,6},{8,11},{9,8},{10,9... | collective-permute-start | bytes 528392 | tf_op jit(solution)/shard_map/ppermute | solution.py:683
  7.7 8.2 %collective-permute-start.1 = (f32[344,128]{1,0:T(8,128)S(1)}, f32[344,128]{1,0:T(8,128)S(1)}, u32[]{:S(2)}, u32[]{:S(2)}) collective-permute-start(f32[344,128]{1,0:T(8,128)S(1)} %get-tuple-element.32), channel_id=1, source_target_pairs={{0,1},{1,2},{2,3},{3,0},{4,5},{5,6},{6,7},{7,4},{8,9},{9,10},{10,1... | collective-permute-start | bytes 528392 | tf_op jit(solution)/shard_map/ppermute | solution.py:683
  7.7 7.1 %collective-permute-start.2 = (f32[8,128]{1,0:T(8,128)S(1)}, f32[8,128]{1,0:T(8,128)S(1)}, u32[]{:S(2)}, u32[]{:S(2)}) collective-permute-start(f32[8,128]{1,0:T(8,128)S(1)} %get-tuple-element.33.refs_3_), channel_id=1, source_target_pairs={{0,2},{1,3},{2,0},{3,1},{4,6},{5,7},{6,4},{7,5},{8,10},{9,11},{10,... | collective-permute-start | bytes 12296 | tf_op jit(solution)/shard_map/ppermute | solution.py:683
  16.0 9.8 %collective-permute-start.3 = (f32[392,128]{1,0:T(8,128)S(1)}, f32[392,128]{1,0:T(8,128)S(1)}, u32[]{:S(2)}, u32[]{:S(2)}) collective-permute-start(f32[392,128]{1,0:T(8,128)S(1)} %shard_map.105.column.charged), channel_id=1, source_target_pairs={{0,4},{4,8},{8,12},{12,16},{16,20},{20,24},{24,28},{28,0},{1,5},{5... | collective-permute-start | bytes 602120 | tf_op jit(solution)/shard_map/ppermute | solution.py:683
  18.2 8.7 %collective-permute-start.4 = (f32[392,128]{1,0:T(8,128)S(1)}, f32[392,128]{1,0:T(8,128)S(1)}, u32[]{:S(2)}, u32[]{:S(2)}) collective-permute-start(f32[392,128]{1,0:T(8,128)S(1)} %shard_map.105.column.charged), channel_id=1, source_target_pairs={{0,28},{4,0},{8,4},{12,8},{16,12},{20,16},{24,20},{28,24},{1,29},{... | collective-permute-start | bytes 602120 | tf_op jit(solution)/shard_map/ppermute | solution.py:683
  20.4 9.6 %collective-permute-start.5 = (f32[368,128]{1,0:T(8,128)S(1)}, f32[368,128]{1,0:T(8,128)S(1)}, u32[]{:S(2)}, u32[]{:S(2)}) collective-permute-start(f32[368,128]{1,0:T(8,128)S(1)} %get-tuple-element.46), channel_id=1, source_target_pairs={{0,4},{4,8},{8,12},{12,16},{16,20},{20,24},{24,28},{28,0},{1,5},{5... | collective-permute-start | bytes 565256 | tf_op jit(solution)/shard_map/ppermute | solution.py:683
  23.1 6.9 %collective-permute-start.6 = (f32[368,128]{1,0:T(8,128)S(1)}, f32[368,128]{1,0:T(8,128)S(1)}, u32[]{:S(2)}, u32[]{:S(2)}) collective-permute-start(f32[368,128]{1,0:T(8,128)S(1)} %get-tuple-element.47), channel_id=1, source_target_pairs={{0,28},{4,0},{8,4},{12,8},{16,12},{20,16},{24,20},{28,24},{1,29},{... | collective-permute-start | bytes 565256 | tf_op jit(solution)/shard_map/ppermute | solution.py:683
  23.1 6.7 %collective-permute-start.7 = (f32[80,128]{1,0:T(8,128)S(1)}, f32[80,128]{1,0:T(8,128)S(1)}, u32[]{:S(2)}, u32[]{:S(2)}) collective-permute-start(f32[80,128]{1,0:T(8,128)S(1)} %get-tuple-element.48), channel_id=1, source_target_pairs={{0,8},{4,12},{8,16},{12,20},{16,24},{20,28},{24,0},{28,4},{1,9},{5... | collective-permute-start | bytes 122888 | tf_op jit(solution)/shard_map/ppermute | solution.py:683
  25.7 4.2 %collective-permute-start.8 = (f32[80,128]{1,0:T(8,128)S(1)}, f32[80,128]{1,0:T(8,128)S(1)}, u32[]{:S(2)}, u32[]{:S(2)}) collective-permute-start(f32[80,128]{1,0:T(8,128)S(1)} %get-tuple-element.49), channel_id=1, source_target_pairs={{0,24},{4,28},{8,0},{12,4},{16,8},{20,12},{24,16},{28,20},{1,25},{... | collective-permute-start | bytes 122888 | tf_op jit(solution)/shard_map/ppermute | solution.py:683
  27.0 3.0 %copy-start = (s32[3,1,1,32,128]{4,3,2,1,0:T(8,128)S(1)}, s32[3,1,1,32,128]{4,3,2,1,0:T(8,128)}, u32[]{:S(2)}) copy-start(s32[3,1,1,32,128]{4,3,2,1,0:T(8,128)} %param.9) | copy-start | bytes 147460
  27.0 3.0 %copy-start.1 = (f32[3,1,1,32,128]{4,3,2,1,0:T(8,128)S(1)}, f32[3,1,1,32,128]{4,3,2,1,0:T(8,128)}, u32[]{:S(2)}) copy-start(f32[3,1,1,32,128]{4,3,2,1,0:T(8,128)} %param.10) | copy-start | bytes 147460
  27.0 3.0 %copy-start.2 = (f32[1,1,32,128]{3,2,1,0:T(8,128)S(1)}, f32[1,1,32,128]{3,2,1,0:T(8,128)}, u32[]{:S(2)}) copy-start(f32[1,1,32,128]{3,2,1,0:T(8,128)} %param.12) | copy-start | bytes 49156
  27.0 3.0 %copy-start.3 = (f32[1,1,32,128]{3,2,1,0:T(8,128)S(1)}, f32[1,1,32,128]{3,2,1,0:T(8,128)}, u32[]{:S(2)}) copy-start(f32[1,1,32,128]{3,2,1,0:T(8,128)} %param.11) | copy-start | bytes 49156
  27.0 3.0 %copy-start.4 = (f32[3,1,1,32,128]{4,3,2,1,0:T(8,128)S(1)}, f32[3,1,1,32,128]{4,3,2,1,0:T(8,128)}, u32[]{:S(2)}) copy-start(f32[3,1,1,32,128]{4,3,2,1,0:T(8,128)} %param.13) | copy-start | bytes 147460
  32.4 10.1 %collective-permute-start.9 = (f32[96,128]{1,0:T(8,128)S(1)}, f32[96,128]{1,0:T(8,128)S(1)}, u32[]{:S(2)}, u32[]{:S(2)}) collective-permute-start(f32[96,128]{1,0:T(8,128)S(1)} %get-tuple-element.50.moved), channel_id=1, source_target_pairs={{0,1},{1,2},{2,3},{3,0},{4,5},{5,6},{6,7},{7,4},{8,9},{9,10},{10,1... | collective-permute-start | bytes 147464 | tf_op jit(solution)/shard_map/ppermute | solution.py:683
  36.0 6.6 %collective-permute-start.10 = (f32[96,128]{1,0:T(8,128)S(1)}, f32[96,128]{1,0:T(8,128)S(1)}, u32[]{:S(2)}, u32[]{:S(2)}) collective-permute-start(f32[96,128]{1,0:T(8,128)S(1)} %get-tuple-element.50.moved), channel_id=1, source_target_pairs={{0,3},{1,0},{2,1},{3,2},{4,7},{5,4},{6,5},{7,6},{8,11},{9,8},{10,9... | collective-permute-start | bytes 147464 | tf_op jit(solution)/shard_map/ppermute | solution.py:683
  38.0 7.3 %collective-permute-start.13 = (f32[96,128]{1,0:T(8,128)S(1)}, f32[96,128]{1,0:T(8,128)S(1)}, u32[]{:S(2)}, u32[]{:S(2)}) collective-permute-start(f32[96,128]{1,0:T(8,128)S(1)} %get-tuple-element.50.moved), channel_id=1, source_target_pairs={{0,4},{4,8},{8,12},{12,16},{16,20},{20,24},{24,28},{28,0},{1,5},{5... | collective-permute-start | bytes 147464 | tf_op jit(solution)/shard_map/ppermute | solution.py:683
  42.5 4.9 %collective-permute-start.14 = (f32[96,128]{1,0:T(8,128)S(1)}, f32[96,128]{1,0:T(8,128)S(1)}, u32[]{:S(2)}, u32[]{:S(2)}) collective-permute-start(f32[96,128]{1,0:T(8,128)S(1)} %get-tuple-element.50.moved), channel_id=1, source_target_pairs={{0,28},{4,0},{8,4},{12,8},{16,12},{20,16},{24,20},{28,24},{1,29},{... | collective-permute-start | bytes 147464 | tf_op jit(solution)/shard_map/ppermute | solution.py:683
  42.6 7.7 %collective-permute-start.11 = (f32[192,128]{1,0:T(8,128)S(1)}, f32[192,128]{1,0:T(8,128)S(1)}, u32[]{:S(2)}, u32[]{:S(2)}) collective-permute-start(f32[192,128]{1,0:T(8,128)S(1)} %constant_dynamic-update-slice_fusion), channel_id=1, source_target_pairs={{0,4},{4,8},{8,12},{12,16},{16,20},{20,24},{24,28},{28,0},{1,5},{5... | collective-permute-start | bytes 294920 | tf_op jit(solution)/shard_map/ppermute | solution.py:683
  45.3 5.0 %collective-permute-start.12 = (f32[192,128]{1,0:T(8,128)S(1)}, f32[192,128]{1,0:T(8,128)S(1)}, u32[]{:S(2)}, u32[]{:S(2)}) collective-permute-start(f32[192,128]{1,0:T(8,128)S(1)} %constant_dynamic-update-slice_fusion), channel_id=1, source_target_pairs={{0,28},{4,0},{8,4},{12,8},{16,12},{20,16},{24,20},{28,24},{1,29},{... | collective-permute-start | bytes 294920 | tf_op jit(solution)/shard_map/ppermute | solution.py:683
